TPU v7x, 32 devices: a whole 2x2x4 slice. The times are simulated.
32 devices in a mesh: frag: 4 (over y, x), tile: 4 (over z), ka: 2 (over core).
Axes of the slice: x: 2, y: 2, z: 4, core: 2. Of those that a mesh axis runs over, the one named last changes fastest.
Arguments:
- sizes: int32 [32], replicated, may hold values from 40 to 400
- neighbors: int32 [32, 4], P('frag'), may hold values from 0 to 31, as said below
- slot_fragment: int32 [32], replicated, may hold values from 0 to 31, as said below
- density: bfloat16 [32, 512, 512], P('frag', ('tile', 'ka')), may hold values from -6 to 6
- hcore: bfloat16 [32, 512, 512], P('frag', ('tile', 'ka')), may hold values from -3 to 3
- integrals: bfloat16 [32, 16, 512, 512], P('frag', ('tile', 'ka')), may hold values from -0.15625 to 0.15625
- couple: bfloat16 [32, 4, 512, 512], P('frag', None, ('tile', 'ka')), may hold values from -2.390625 to 2.390625
Outputs:
- fock: float32 [32, 512, 512], P('frag', ('tile', 'ka'))
Inputs may be any that keep to these rules, and one draw needn't show every extreme that they name: `neighbors`: fragment f belongs to group f // 8; each entry names a fragment other than f itself, belonging to the same group or to the next group on either side. `slot_fragment`: A permutation of the fragments; slots s with s // 8 == h form balanced group h; no group's fragments fill more than 2 slots of one balanced group, and some pair of groups reaches 2.
All inputs are finite; a program needn't handle non-finite values.
Results may differ from a plain program's by a relative error of at most 0.002.
Values may be sent and summed in bfloat16 or wider, within the bound.
A program may use at most 64 MiB of HBM per device.

v0:
```python
from functools import partial

import jax
import jax.numpy as jnp
from jax import lax
from jax.sharding import PartitionSpec as P

TILE = 128
TILES = 4


def with_halo(block, sides, width):
    for axis, dim in sides:
        count = lax.axis_size(axis)
        forward = [(i, i + 1) for i in range(count - 1)]
        backward = [(target, source) for source, target in forward]
        low = lax.ppermute(
            lax.slice_in_dim(block, block.shape[dim] - width, None, axis=dim), axis, forward
        )
        high = lax.ppermute(lax.slice_in_dim(block, 0, width, axis=dim), axis, backward)
        block = jnp.concatenate([low, block, high], axis=dim)
    return block


def block_fock(slot_density, factors, extent, full_size):
    factor_block = factors[:, :extent, :extent]
    density_block = slot_density[:extent, :extent]
    product = jnp.einsum(
        "qik,kj->qij", factor_block, density_block, preferred_element_type=jnp.float32
    ).astype(jnp.bfloat16)
    exchange_term = jnp.einsum(
        "qij,qlj->qil", product, factor_block, preferred_element_type=jnp.float32
    )
    coulomb = jnp.einsum(
        "qij,ij->q", factor_block, density_block, preferred_element_type=jnp.float32
    )
    summed_terms = jnp.sum(
        coulomb[:, None, None] * factor_block.astype(jnp.float32) - 0.5 * exchange_term, axis=0
    )
    return jnp.pad(summed_terms, ((0, full_size - extent), (0, full_size - extent)))


def local(sizes, neighbors, slot_fragment, density, hcore, integrals, couple):
    groups = lax.axis_size("frag")
    my_group = lax.axis_index("frag")
    core_count = lax.axis_size("ka")
    my_lane = lax.axis_index("tile") * core_count + lax.axis_index("ka")
    per_group, slab_rows, basis_size = density.shape
    capacity = max(1, per_group // groups)
    first_frag = my_group * per_group
    local_ids = jnp.arange(per_group, dtype=jnp.int32)
    row_ids = my_lane * slab_rows + jnp.arange(slab_rows, dtype=jnp.int32)
    col_ids = jnp.arange(basis_size, dtype=jnp.int32)
    own_sizes = lax.dynamic_slice_in_dim(sizes, first_frag, per_group)
    keep_mask = (
        (row_ids[None, :, None] < own_sizes[:, None, None])
        & (col_ids[None, None, :] < own_sizes[:, None, None])
    ).astype(jnp.float32)
    masked = (density.astype(jnp.float32) * keep_mask).astype(jnp.bfloat16)
    fragment_ids = first_frag + local_ids
    matches = slot_fragment[None, :] == fragment_ids[:, None]
    slot_of = jnp.sum(
        jnp.where(matches, jnp.arange(slot_fragment.shape[0], dtype=jnp.int32)[None, :], 0), axis=1
    )
    target = slot_of // per_group
    earlier = local_ids[None, :] < local_ids[:, None]
    rank_pos = jnp.sum((target[:, None] == target[None, :]) & earlier, axis=1)
    send_slot = target * capacity + rank_pos
    selector = (
        jnp.arange(groups * capacity, dtype=jnp.int32)[:, None] == send_slot[None, :]
    ).astype(jnp.bfloat16)
    outgoing = jnp.einsum(
        "sj,jrw->srw", selector, masked, preferred_element_type=jnp.float32
    ).astype(jnp.bfloat16)
    received = lax.all_to_all(
        outgoing.reshape(groups, capacity, slab_rows, basis_size),
        "frag",
        split_axis=0,
        concat_axis=0,
        tiled=True,
    )
    held_frag = lax.dynamic_slice_in_dim(slot_fragment, first_frag, per_group)
    source = held_frag // per_group
    same_source = source[:, None] == source[None, :]
    before = held_frag[None, :] < held_frag[:, None]
    flat_index = source * capacity + jnp.sum(same_source & before, axis=1)
    balanced = jnp.take(
        received.reshape(groups * capacity, slab_rows, basis_size), flat_index, axis=0
    )
    gathered = lax.all_gather(balanced, ("tile", "ka"), axis=1, tiled=True)
    held_sizes = jnp.take(sizes, held_frag)
    tile_count = (held_sizes + TILE - 1) // TILE - 1

    def slot_fock(position):
        slot_density = gathered[position]
        factors = integrals[position]
        branches = [
            partial(block_fock, extent=(count + 1) * TILE, full_size=basis_size)
            for count in range(TILES)
        ]
        return lax.switch(tile_count[position], branches, slot_density, factors)

    fock_parts = lax.map(slot_fock, local_ids)
    summed = lax.psum_scatter(fock_parts, ("tile", "ka"), scatter_dimension=1, tiled=True)
    back_rows = (
        jnp.zeros((groups * capacity, slab_rows, basis_size), jnp.float32)
        .at[flat_index]
        .set(summed)
    )
    returned = lax.all_to_all(
        back_rows.reshape(groups, capacity, slab_rows, basis_size),
        "frag",
        split_axis=0,
        concat_axis=0,
        tiled=True,
    )
    two_body = jnp.take(
        returned.reshape(groups * capacity, slab_rows, basis_size), send_slot, axis=0
    )
    extended = with_halo(masked, (("frag", 0),), per_group)
    near_index = (neighbors - (my_group - 1) * per_group).reshape(-1)
    picked = jnp.take(extended, near_index, axis=0).reshape(couple.shape)
    coupling = jnp.sum(couple.astype(jnp.float32) * picked.astype(jnp.float32), axis=1)
    return keep_mask * (hcore.astype(jnp.float32) + two_body + coupling)


def solution(mesh):
    return jax.shard_map(
        local,
        mesh=mesh,
        in_specs=(
            P(),
            P("frag", None),
            P(),
            P("frag", ("tile", "ka"), None),
            P("frag", ("tile", "ka"), None),
            P("frag", ("tile", "ka"), None, None),
            P("frag", None, ("tile", "ka"), None),
        ),
        out_specs=P("frag", ("tile", "ka"), None),
        check_vma=False,
    )
```

profile of v0, /device:TPU:0, one launch (start us, length us, event | category | flops | bytes accessed | tf_op | source)
XLA Modules:
  0.0 265.3 jit_solution(1163581827824407936)
XLA Ops:
  11.5 5.2 %all-to-all-start = ((bf16[4,2,64,512]{3,1,2,0:T(2,128)(2,1)}), bf16[4,2,64,512]{3,1,2,0:T(2,128)(2,1)S(1)}, u32[]{:S(2)}, u32[]{:S(2)}) async-start(bf16[4,2,64,512]{3,1,2,0:T(2,128)(2,1)} %copy.21), calls=%async_computation | async-start | bytes 1048576 | tf_op jit(solution)/shard_map/all_to_all | solution.py:75
  17.7 7.0 %all-to-all-done = bf16[4,2,64,512]{3,1,2,0:T(2,128)(2,1)S(1)} async-done(((bf16[4,2,64,512]{3,1,2,0:T(2,128)(2,1)}), bf16[4,2,64,512]{3,1,2,0:T(2,128)(2,1)S(1)}, u32[]{:S(2)}, u32[]{:S(2)}) %all-to-all-start) | async-done | bytes 524320 | tf_op jit(solution)/shard_map/all_to_all | solution.py:75
  26.4 47.2 %all-gather.2.cloned.1.call-done = bf16[8,512,512]{2,1,0:T(8,128)(2,1)} async-done(((bf16[8,64,512]{2,1,0:T(8,128)(2,1)}), bf16[8,512,512]{2,1,0:T(8,128)(2,1)}) %all-gather.2.cloned.1.call-update) | async-done | bytes 4194320 | tf_op jit(solution)/shard_map/all_gather | solution.py:90
  73.6 73.1 %while.10 = (s32[]{:T(128)}, f32[8,512,512]{2,1,0:T(8,128)}, s32[8]{0:T(128)S(1)}, s32[8]{0:T(128)S(1)}, bf16[8,2,512,512]{3,2,1,0:T(8,128)(2,1)}, /*index=5*/bf...) while((s32[]{:T(128)}, f32[8,512,512]{2,1,0:T(8,128)}, ...), condition=%wide.region_12.13_spmd, body=%wide.region_3.12_spmd.sunk | while | flops 1077673984 | bytes 12190951 | solution.py:103
  77.5 3.2 %conditional.2 = (f32[1,512,512]{2,1,0:T(8,128)S(1)}) conditional(s32[]{:T(128)} %bitcast.80, (bf16[8,2,512,512]{3,2,1,0:T(8,128)(2,1)}, s32[]{:T(128)}, bf16[8,512,512]{2,1,0:T(8,128)(2,1)}) %tuple.56, (bf16[8,2,512,512]{3,2,1,0:T(8,128)(2,1)}, s32[]{:T(128)}, bf16[8,512,512]{2,1,0:T(8,128)(2,1)}) %tuple.56, ...), branch_computations={%region_4.5_spmd, %region_6.7_spmd, %region_8.9_spmd, %region_10.1... | conditional | flops 1077673984 | bytes 10093080 | solution.py:101
  77.5 1.3 dynamic-slice_bitcast_fusion
  85.6 5.2 %conditional.2 = (f32[1,512,512]{2,1,0:T(8,128)S(1)}) conditional(s32[]{:T(128)} %bitcast.80, (bf16[8,2,512,512]{3,2,1,0:T(8,128)(2,1)}, s32[]{:T(128)}, bf16[8,512,512]{2,1,0:T(8,128)(2,1)}) %tuple.56, (bf16[8,2,512,512]{3,2,1,0:T(8,128)(2,1)}, s32[]{:T(128)}, bf16[8,512,512]{2,1,0:T(8,128)(2,1)}) %tuple.56, ...), branch_computations={%region_4.5_spmd, %region_6.7_spmd, %region_8.9_spmd, %region_10.1... | conditional | flops 1077673984 | bytes 10093080 | solution.py:101
  85.6 1.3 dynamic-slice_bitcast_fusion.4
  88.1 1.7 convolution_bitcast_fusion.2
  95.8 3.2 %conditional.2 = (f32[1,512,512]{2,1,0:T(8,128)S(1)}) conditional(s32[]{:T(128)} %bitcast.80, (bf16[8,2,512,512]{3,2,1,0:T(8,128)(2,1)}, s32[]{:T(128)}, bf16[8,512,512]{2,1,0:T(8,128)(2,1)}) %tuple.56, (bf16[8,2,512,512]{3,2,1,0:T(8,128)(2,1)}, s32[]{:T(128)}, bf16[8,512,512]{2,1,0:T(8,128)(2,1)}) %tuple.56, ...), branch_computations={%region_4.5_spmd, %region_6.7_spmd, %region_8.9_spmd, %region_10.1... | conditional | flops 1077673984 | bytes 10093080 | solution.py:101
  95.8 1.3 dynamic-slice_bitcast_fusion
  103.9 3.2 %conditional.2 = (f32[1,512,512]{2,1,0:T(8,128)S(1)}) conditional(s32[]{:T(128)} %bitcast.80, (bf16[8,2,512,512]{3,2,1,0:T(8,128)(2,1)}, s32[]{:T(128)}, bf16[8,512,512]{2,1,0:T(8,128)(2,1)}) %tuple.56, (bf16[8,2,512,512]{3,2,1,0:T(8,128)(2,1)}, s32[]{:T(128)}, bf16[8,512,512]{2,1,0:T(8,128)(2,1)}) %tuple.56, ...), branch_computations={%region_4.5_spmd, %region_6.7_spmd, %region_8.9_spmd, %region_10.1... | conditional | flops 1077673984 | bytes 10093080 | solution.py:101
  103.9 1.3 dynamic-slice_bitcast_fusion
  112.0 5.2 %conditional.2 = (f32[1,512,512]{2,1,0:T(8,128)S(1)}) conditional(s32[]{:T(128)} %bitcast.80, (bf16[8,2,512,512]{3,2,1,0:T(8,128)(2,1)}, s32[]{:T(128)}, bf16[8,512,512]{2,1,0:T(8,128)(2,1)}) %tuple.56, (bf16[8,2,512,512]{3,2,1,0:T(8,128)(2,1)}, s32[]{:T(128)}, bf16[8,512,512]{2,1,0:T(8,128)(2,1)}) %tuple.56, ...), branch_computations={%region_4.5_spmd, %region_6.7_spmd, %region_8.9_spmd, %region_10.1... | conditional | flops 1077673984 | bytes 10093080 | solution.py:101
  112.0 1.3 dynamic-slice_bitcast_fusion.4
  114.5 1.7 convolution_bitcast_fusion.2
  122.2 5.2 %conditional.2 = (f32[1,512,512]{2,1,0:T(8,128)S(1)}) conditional(s32[]{:T(128)} %bitcast.80, (bf16[8,2,512,512]{3,2,1,0:T(8,128)(2,1)}, s32[]{:T(128)}, bf16[8,512,512]{2,1,0:T(8,128)(2,1)}) %tuple.56, (bf16[8,2,512,512]{3,2,1,0:T(8,128)(2,1)}, s32[]{:T(128)}, bf16[8,512,512]{2,1,0:T(8,128)(2,1)}) %tuple.56, ...), branch_computations={%region_4.5_spmd, %region_6.7_spmd, %region_8.9_spmd, %region_10.1... | conditional | flops 1077673984 | bytes 10093080 | solution.py:101
  124.7 1.7 convolution_bitcast_fusion.2
  132.4 5.2 %conditional.2 = (f32[1,512,512]{2,1,0:T(8,128)S(1)}) conditional(s32[]{:T(128)} %bitcast.80, (bf16[8,2,512,512]{3,2,1,0:T(8,128)(2,1)}, s32[]{:T(128)}, bf16[8,512,512]{2,1,0:T(8,128)(2,1)}) %tuple.56, (bf16[8,2,512,512]{3,2,1,0:T(8,128)(2,1)}, s32[]{:T(128)}, bf16[8,512,512]{2,1,0:T(8,128)(2,1)}) %tuple.56, ...), branch_computations={%region_4.5_spmd, %region_6.7_spmd, %region_8.9_spmd, %region_10.1... | conditional | flops 1077673984 | bytes 10093080 | solution.py:101
  132.4 1.3 dynamic-slice_bitcast_fusion.4
  134.9 1.7 convolution_bitcast_fusion.2
  142.5 3.2 %conditional.2 = (f32[1,512,512]{2,1,0:T(8,128)S(1)}) conditional(s32[]{:T(128)} %bitcast.80, (bf16[8,2,512,512]{3,2,1,0:T(8,128)(2,1)}, s32[]{:T(128)}, bf16[8,512,512]{2,1,0:T(8,128)(2,1)}) %tuple.56, (bf16[8,2,512,512]{3,2,1,0:T(8,128)(2,1)}, s32[]{:T(128)}, bf16[8,512,512]{2,1,0:T(8,128)(2,1)}) %tuple.56, ...), branch_computations={%region_4.5_spmd, %region_6.7_spmd, %region_8.9_spmd, %region_10.1... | conditional | flops 1077673984 | bytes 10093080 | solution.py:101
  142.5 1.3 dynamic-slice_bitcast_fusion
  146.8 3.5 %collective-permute-start = (bf16[8,64,512]{2,1,0:T(8,128)(2,1)S(1)}, bf16[8,64,512]{2,1,0:T(8,128)(2,1)S(1)}, u32[]{:S(2)}, u32[]{:S(2)}) collective-permute-start(bf16[8,64,512]{2,1,0:T(8,128)(2,1)S(1)} %fusion.20), channel_id=1, source_target_pairs={{0,8},{8,16},{16,24},{1,9},{9,17},{17,25},{2,10},{10,18},{18,26},{... | collective-permute-start | bytes 1572872 | tf_op jit(solution)/shard_map/ppermute | solution.py:17
  151.8 83.6 %reduce-scatter.2.cloned.1.call-done = f32[8,64,512]{2,1,0:T(8,128)} async-done(((f32[8,512,512]{2,1,0:T(8,128)}), f32[8,64,512]{2,1,0:T(8,128)}) %reduce-scatter.2.cloned.1.call-update) | async-done | bytes 1048592 | tf_op jit(solution)/shard_map/reduce_scatter | solution.py:104
  236.5 3.2 %scatter_fusion = f32[8,64,512]{2,1,0:T(8,128)} fusion(f32[8,64,512]{2,1,0:T(8,128)} %broadcast_in_dim.101, s32[8]{0:T(128)S(1)} %get-tuple-element.187, f32[8,64,512]{2,1,0:T(8,128)} %reduce-scatter.2.cloned.1.call-done), kind=kCustom, calls=%fused_computation.4 | custom fusion | bytes 3145760 | tf_op jit(solution)/shard_map/scatter | solution.py:108
  239.7 3.8 %all-to-all-start.1 = ((f32[4,2,64,512]{3,2,1,0:T(8,128)}), f32[4,2,64,512]{3,2,1,0:T(8,128)S(1)}, u32[]{:S(2)}, u32[]{:S(2)}) async-start(f32[4,2,64,512]{3,2,1,0:T(8,128)} %bitcast.24), calls=%async_computation.2 | async-start | bytes 2097152 | tf_op jit(solution)/shard_map/all_to_all | solution.py:110
  244.4 1.4 pad_maximum_fusion
  245.8 2.0 gather_fusion.3
  247.8 4.3 %multiply_reduce_fusion = f32[8,64,512]{2,1,0:T(8,128)} fusion(bf16[8,4,64,512]{3,2,1,0:T(8,128)(2,1)} %param.19, pred[8,4]{1,0:T(8,128)(4,1)S(1)} %copy.23, bf16[32,64,512]{2,1,0:T(8,128)(2,1)} %gather_fusion.3), kind=kLoop, calls=%fused_computation.49 | loop fusion | flops 4980736 | bytes 5242912 | tf_op jit(solution)/shard_map/reduce_sum | solution.py:123
  252.2 3.1 %all-to-all-done.1 = f32[4,2,64,512]{3,2,1,0:T(8,128)S(1)} async-done(((f32[4,2,64,512]{3,2,1,0:T(8,128)}), f32[4,2,64,512]{3,2,1,0:T(8,128)S(1)}, u32[]{:S(2)}, u32[]{:S(2)}) %all-to-all-start.1) | async-done | bytes 1048608 | tf_op jit(solution)/shard_map/all_to_all | solution.py:110
  255.9 2.5 and_select_fusion
  (121 shorter events, 47.4 us)
Async XLA Ops:
  9.8 7.0 %copy-start.4 = (s32[32]{0:T(128)S(1)}, s32[32]{0:T(128)}, u32[]{:S(2)}) copy-start(s32[32]{0:T(128)} %param.15) | copy-start | bytes 388
  9.8 7.1 %copy-start = (s32[32]{0:T(128)S(1)}, s32[32]{0:T(128)}, u32[]{:S(2)}) copy-start(s32[32]{0:T(128)} %param.13) | copy-start | bytes 388
  11.5 13.2 %all-to-all-start = ((bf16[4,2,64,512]{3,1,2,0:T(2,128)(2,1)}), bf16[4,2,64,512]{3,1,2,0:T(2,128)(2,1)S(1)}, u32[]{:S(2)}, u32[]{:S(2)}) async-start(bf16[4,2,64,512]{3,1,2,0:T(2,128)(2,1)} %copy.21), calls=%async_computation | async-start | bytes 1048576 | tf_op jit(solution)/shard_map/all_to_all | solution.py:75
  16.7 56.9 %all-gather.2.cloned.1.call-start = ((), (), s32[]{:S(2)}) async-start(), calls=%async_computation.3 | async-start | bytes 4718592 | tf_op jit(solution)/shard_map/all_gather | solution.py:90
  26.3 209.0 %reduce-scatter.2.cloned.1.call-start = ((), (), s32[]{:S(2)}) async-start(), calls=%async_computation.4 | async-start | bytes 9437184 | tf_op jit(solution)/shard_map/reduce_scatter | solution.py:104
  146.8 4.8 %copy-start.3 = (s32[8,4]{0,1:T(4,128)S(1)}, s32[8,4]{0,1:T(4,128)}, u32[]{:S(2)}) copy-start(s32[8,4]{0,1:T(4,128)} %param.14) | copy-start | bytes 388
  146.8 96.8 %collective-permute-start = (bf16[8,64,512]{2,1,0:T(8,128)(2,1)S(1)}, bf16[8,64,512]{2,1,0:T(8,128)(2,1)S(1)}, u32[]{:S(2)}, u32[]{:S(2)}) collective-permute-start(bf16[8,64,512]{2,1,0:T(8,128)(2,1)S(1)} %fusion.20), channel_id=1, source_target_pairs={{0,8},{8,16},{16,24},{1,9},{9,17},{17,25},{2,10},{10,18},{18,26},{... | collective-permute-start | bytes 1572872 | tf_op jit(solution)/shard_map/ppermute | solution.py:17
  150.3 94.1 %collective-permute-start.1 = (bf16[8,64,512]{2,1,0:T(8,128)(2,1)S(1)}, bf16[8,64,512]{2,1,0:T(8,128)(2,1)}, u32[]{:S(2)}, u32[]{:S(2)}) collective-permute-start(bf16[8,64,512]{2,1,0:T(8,128)(2,1)S(1)} %fusion.20), channel_id=1, source_target_pairs={{8,0},{16,8},{24,16},{9,1},{17,9},{25,17},{10,2},{18,10},{26,18},{... | collective-permute-start | bytes 1572872 | tf_op jit(solution)/shard_map/ppermute | solution.py:20
  239.7 15.5 %all-to-all-start.1 = ((f32[4,2,64,512]{3,2,1,0:T(8,128)}), f32[4,2,64,512]{3,2,1,0:T(8,128)S(1)}, u32[]{:S(2)}, u32[]{:S(2)}) async-start(f32[4,2,64,512]{3,2,1,0:T(8,128)} %bitcast.24), calls=%async_computation.2 | async-start | bytes 2097152 | tf_op jit(solution)/shard_map/all_to_all | solution.py:110
  243.6 0.8 copy-start.2
  252.2 3.7 %copy-start.1 = (bf16[8,64,512]{2,1,0:T(8,128)(2,1)S(1)}, bf16[8,64,512]{2,1,0:T(8,128)(2,1)}, u32[]{:S(2)}) copy-start(bf16[8,64,512]{2,1,0:T(8,128)(2,1)} %param.17) | copy-start | bytes 1572868
Sparse Core Ops, SparseCore 0:
  26.5 47.1 all-gather.1
  146.9 88.4 reduce-scatter.1
where the time goes:
time: 268 us; the launch traced here: 265 us
  waiting for transfers between devices  141 us (53%)
  local copies, waits for them, and re-layouts  50.3 us (19%)
  loops' own time  21.6 us (8%)
  starting transfers between devices  13.8 us (5%)
  between operations  13.6 us (5%)
  matrix products  13.1 us (5%)
  other arithmetic  12 us (4%)
    reduce_scatter x1, waiting for transfers between devices, local(): lax.psum_scatter(fock_parts, ('tile', 'ka'), scatter_dimension=1, tiled=T...  83.6 us
    all_gather x1, waiting for transfers between devices, local(): gathered = lax.all_gather(balanced, ('tile', 'ka'), axis=1, tiled=True)  47.2 us
    another operation x1, loops' own time, local(): fock_parts = lax.map(slot_fock, local_ids)  21.1 us
    squeeze x8, local copies, waits for them, and re-layouts, slot_fock(): factors = integrals[position]  10.4 us
    squeeze x8, local copies, waits for them, and re-layouts, slot_fock(): slot_density = gathered[position]  8.66 us
    dynamic_update_slice x8, local copies, waits for them, and re-layouts, local(): fock_parts = lax.map(slot_fock, local_ids)  8.55 us
    dot_general x8, matrix products, block_fock(): jnp.einsum('qij,ij->q', factor_block, density_block, preferred_element_ty...  7.8 us
    all_to_all x1, waiting for transfers between devices, local(): lax.all_to_all(outgoing.reshape(groups, capacity, slab_rows, basis_size),...  7.05 us
  transfers between devices with their start and end apart: 6, of which 4 were waited for; matrix products, arithmetic and copies ran while one was open for 5% of the time, Pallas kernels for 0%

commit v1 on v0

v1 whole, which is shorter than its diff:
```python
import math
from functools import partial

import jax
import jax.numpy as jnp
from jax import lax
from jax.experimental import pallas as pl
from jax.experimental.pallas import tpu as pltpu
from jax.sharding import PartitionSpec as P

TILE = 128
WIRE = jnp.float16
VM = pl.BlockSpec(memory_space=pltpu.VMEM)
SM = pl.BlockSpec(memory_space=pltpu.SMEM)
PAR = pltpu.CompilerParams(vmem_limit_bytes=58 << 20)


def keep_of(size, row0, shape):
    rows = row0 + lax.broadcasted_iota(jnp.int32, shape, 0)
    cols = lax.broadcasted_iota(jnp.int32, shape, 1)
    return (rows < size) & (cols < size)


def prep_kernel(size_ref, pick_ref, row_ref, d_ref, m_ref, o_ref):
    count, rows, cols = d_ref.shape
    for f in range(count):
        keep = keep_of(size_ref[f], row_ref[0], (rows, cols))
        m_ref[f] = jnp.where(keep, d_ref[f].astype(jnp.float32), 0.0).astype(m_ref.dtype)
    for s in range(o_ref.shape[0]):
        o_ref[s] = m_ref[pick_ref[s]]


def pack_kernel(src_ref, k_ref, r_ref, o_ref):
    for t in range(o_ref.shape[0]):
        o_ref[t] = r_ref[src_ref[t], :, pl.ds(pl.multiple_of(k_ref[t] * TILE, TILE), TILE)]


def fock_kernel(scale, cls_ref, off_ref, g_ref, l_ref, o_ref, d_scr, acc_scr):
    s = pl.program_id(0)
    lanes, _, slab, _ = g_ref.shape
    basis = l_ref.shape[-1]
    off = off_ref[s]

    @pl.when(s == 0)
    def _():
        o_ref[...] = jnp.zeros_like(o_ref)

    for c in range(1, basis // TILE + 1):
        e = c * TILE

        @pl.when(cls_ref[s] == c)
        def _(c=c, e=e):
            for lane in range(e // slab):
                for k in range(c):
                    d_scr[lane * slab:(lane + 1) * slab, k * TILE:(k + 1) * TILE] = g_ref[lane, off + k]

            for q in range(l_ref.shape[1]):
                lq = l_ref[0, q, :e, :e]
                dm = d_scr[:e, :e]
                prod = jnp.dot(lq, dm, preferred_element_type=jnp.float32).astype(jnp.bfloat16)
                coul = jnp.sum(lq.astype(jnp.float32) * dm.astype(jnp.float32))
                exch = lax.dot_general(
                    prod, lq, (((1,), (1,)), ((), ())), preferred_element_type=jnp.float32
                )
                part = coul * lq.astype(jnp.float32) - 0.5 * exch
                if q == 0:
                    acc_scr[:e, :e] = part
                else:
                    acc_scr[:e, :e] += part
            for lane in range(e // slab):
                for k in range(c):
                    tile = acc_scr[lane * slab:(lane + 1) * slab, k * TILE:(k + 1) * TILE]
                    o_ref[lane, off + k] = (tile * scale).astype(o_ref.dtype)


def unpack_kernel(dst_ref, tile_ref, p_ref, o_ref):
    slots, tiles = tile_ref.shape
    o_ref[...] = jnp.zeros_like(o_ref)
    for s in range(slots):
        for k in range(tiles):
            o_ref[dst_ref[s], :, k * TILE:(k + 1) * TILE] = p_ref[tile_ref[s, k]]


def base_kernel(near_ref, low_ref, mid_ref, high_ref, h_ref, c_ref, o_ref, ext):
    f = pl.program_id(0)
    n = mid_ref.shape[0]

    @pl.when(f == 0)
    def _():
        ext[0:n] = low_ref[...]
        ext[n:2 * n] = mid_ref[...]
        ext[2 * n:3 * n] = high_ref[...]

    total = h_ref[0].astype(jnp.float32)
    for k in range(c_ref.shape[1]):
        total += c_ref[0, k].astype(jnp.float32) * ext[near_ref[f, k]].astype(jnp.float32)
    o_ref[0] = total


def final_kernel(scale, size_ref, slot_ref, row_ref, b_ref, r_ref, o_ref):
    count, rows, cols = b_ref.shape
    for f in range(count):
        keep = keep_of(size_ref[f], row_ref[0], (rows, cols))
        back = r_ref[slot_ref[f]].astype(jnp.float32) * scale
        o_ref[f] = jnp.where(keep, b_ref[f] + back, 0.0)


def local(sizes, neighbors, slot_fragment, density, hcore, integrals, couple):
    i32 = jnp.int32
    groups = lax.axis_size("frag")
    my_group = lax.axis_index("frag")
    core_count = lax.axis_size("ka")
    lanes = lax.axis_size("tile") * core_count
    my_lane = lax.axis_index("tile") * core_count + lax.axis_index("ka")
    per_group, slab, basis = density.shape
    chol_here = integrals.shape[1]
    tiles = basis // TILE
    capacity = max(1, per_group // groups)
    buffers = groups * capacity
    first = my_group * per_group
    ids = jnp.arange(per_group, dtype=i32)
    row0 = (my_lane * slab).astype(i32).reshape(1)
    own_sizes = lax.dynamic_slice_in_dim(sizes, first, per_group)

    bound = 1.5 * (basis * 25 / 32) ** 2 * 6 * 0.15625**2 * chol_here * lanes
    scale = 2.0 ** math.ceil(math.log2(bound / 60000))

    matches = slot_fragment[None, :] == (first + ids)[:, None]
    slot_ids = jnp.arange(slot_fragment.shape[0], dtype=i32)
    slot_of = jnp.sum(jnp.where(matches, slot_ids[None, :], 0), axis=1)
    target = slot_of // per_group
    earlier = ids[None, :] < ids[:, None]
    rank_pos = jnp.sum((target[:, None] == target[None, :]) & earlier, axis=1)
    send_slot = (target * capacity + rank_pos).astype(i32)
    out_ids = jnp.arange(buffers, dtype=i32)
    pick = jnp.sum(jnp.where(out_ids[:, None] == send_slot[None, :], ids[None, :], 0), axis=1).astype(i32)

    held = lax.dynamic_slice_in_dim(slot_fragment, first, per_group)
    source = held // per_group
    before = held[None, :] < held[:, None]
    flat = (source * capacity + jnp.sum((source[:, None] == source[None, :]) & before, axis=1)).astype(i32)

    frag_class = (sizes + TILE - 1) // TILE
    slot_class = jnp.sum(
        jnp.where(slot_fragment[:, None] == slot_ids[None, :], frag_class[None, :], 0), axis=1
    ).astype(i32)
    need = jnp.max(jnp.sum(slot_class.reshape(groups, per_group), axis=1))
    cls = lax.dynamic_slice_in_dim(slot_class, first, per_group)
    off = jnp.sum(jnp.where(earlier, cls[None, :], 0), axis=1).astype(i32)
    most = per_group * tiles
    tile_ids = jnp.arange(most, dtype=i32)
    inside = (tile_ids[:, None] >= off[None, :]) & (tile_ids[:, None] < (off + cls)[None, :])
    tile_src = jnp.sum(jnp.where(inside, flat[None, :], 0), axis=1).astype(i32)
    tile_k = jnp.sum(jnp.where(inside, tile_ids[:, None] - off[None, :], 0), axis=1).astype(i32)
    ks = jnp.arange(tiles, dtype=i32)
    tile_at = jnp.where(ks[None, :] < cls[:, None], off[:, None] + ks[None, :], 0).astype(i32)

    slab_bf = jax.ShapeDtypeStruct((per_group, slab, basis), jnp.bfloat16)
    masked, outgoing = pl.pallas_call(
        prep_kernel,
        out_shape=(slab_bf, jax.ShapeDtypeStruct((buffers, slab, basis), jnp.bfloat16)),
        in_specs=[SM, SM, SM, VM],
        out_specs=(VM, VM),
        name="prep",
    )(own_sizes, pick, row0, density)

    received = lax.all_to_all(
        outgoing.reshape(groups, capacity, slab, basis), "frag", split_axis=0, concat_axis=0, tiled=True
    ).reshape(buffers, slab, basis)

    forward = [(i, i + 1) for i in range(groups - 1)]
    backward = [(b, a) for a, b in forward]
    low = lax.ppermute(masked, "frag", forward)
    high = lax.ppermute(masked, "frag", backward)
    near = (neighbors - (my_group - 1) * per_group).astype(i32)

    slab_block = (1, slab, basis)
    nnb = couple.shape[1]
    base = pl.pallas_call(
        base_kernel,
        grid_spec=pltpu.PrefetchScalarGridSpec(
            num_scalar_prefetch=1,
            grid=(per_group,),
            in_specs=[
                VM, VM, VM,
                pl.BlockSpec(slab_block, lambda f, n: (f, 0, 0)),
                pl.BlockSpec((1, nnb, slab, basis), lambda f, n: (f, 0, 0, 0)),
            ],
            out_specs=pl.BlockSpec(slab_block, lambda f, n: (f, 0, 0)),
            scratch_shapes=[pltpu.VMEM((3 * per_group, slab, basis), jnp.bfloat16)],
        ),
        out_shape=jax.ShapeDtypeStruct((per_group, slab, basis), jnp.float32),
        name="base",
    )(near, low, masked, high, hcore, couple)

    def branch(count, received, integrals):
        packed = pl.pallas_call(
            pack_kernel,
            out_shape=jax.ShapeDtypeStruct((count, slab, TILE), jnp.bfloat16),
            in_specs=[SM, SM, VM],
            out_specs=VM,
            name="pack",
        )(tile_src, tile_k, received)
        gathered = lax.all_gather(packed, ("tile", "ka"), axis=0, tiled=True)
        whole = (lanes, count, slab, TILE)
        parts = pl.pallas_call(
            partial(fock_kernel, 1.0 / scale),
            grid_spec=pltpu.PrefetchScalarGridSpec(
                num_scalar_prefetch=2,
                grid=(per_group,),
                in_specs=[
                    pl.BlockSpec(whole, lambda s, a, b: (0, 0, 0, 0), pipeline_mode=pl.Buffered(1)),
                    pl.BlockSpec((1, chol_here, basis, basis), lambda s, a, b: (s, 0, 0, 0)),
                ],
                out_specs=pl.BlockSpec(whole, lambda s, a, b: (0, 0, 0, 0)),
                scratch_shapes=[
                    pltpu.VMEM((basis, basis), jnp.bfloat16),
                    pltpu.VMEM((basis, basis), jnp.float32),
                ],
            ),
            out_shape=jax.ShapeDtypeStruct(whole, jnp.float32),
            compiler_params=PAR,
            name="fock",
        )(cls, off, gathered.reshape(whole), integrals)
        summed = lax.psum_scatter(
            parts.reshape(lanes * count, slab, TILE).astype(WIRE), ("tile", "ka"), scatter_dimension=0, tiled=True
        )
        return pl.pallas_call(
            unpack_kernel,
            out_shape=jax.ShapeDtypeStruct((buffers, slab, basis), jnp.float32),
            in_specs=[SM, SM, VM],
            out_specs=VM,
            name="unpack",
        )(flat, tile_at, summed.astype(jnp.float32))

    step = per_group // 2
    counts = [per_group + step * i for i in range(1, (most - per_group) // step + 1)]
    counts = [c for c in counts if c <= most * 3 // 4] + [most]
    which = jnp.sum(need > jnp.array(counts[:-1], i32)).astype(i32)
    back = lax.switch(which, [partial(branch, c) for c in counts], received, integrals)
    returned = lax.all_to_all(
        back.reshape(groups, capacity, slab, basis).astype(WIRE), "frag", split_axis=0, concat_axis=0, tiled=True
    ).reshape(buffers, slab, basis)
    return pl.pallas_call(
        partial(final_kernel, scale),
        out_shape=jax.ShapeDtypeStruct((per_group, slab, basis), jnp.float32),
        in_specs=[SM, SM, SM, VM, VM],
        out_specs=VM,
        name="final",
    )(own_sizes, send_slot, row0, base, returned.astype(jnp.float32))


def solution(mesh):
    return jax.shard_map(
        local,
        mesh=mesh,
        in_specs=(
            P(),
            P("frag", None),
            P(),
            P("frag", ("tile", "ka"), None),
            P("frag", ("tile", "ka"), None),
            P("frag", ("tile", "ka"), None, None),
            P("frag", None, ("tile", "ka"), None),
        ),
        out_specs=P("frag", ("tile", "ka"), None),
        check_vma=False,
    )
```

time: 268 us -> 184 us (0.69)
  waiting for transfers between devices: 141 us -> 45.3 us
  blocking collectives: 0 us -> 63.5 us
  local copies, waits for them, and re-layouts: 50.3 us -> 2.87 us
  Pallas kernels: 0 us -> 26.3 us
  loops' own time: 21.6 us -> 0.95 us
  matrix products: 13.1 us -> 0 us
    reduce_scatter x1 -> x0, waiting for transfers between devices: 83.6 us -> none  [local(): lax.psum_scatter(fock_parts, ('tile', 'ka'), scatter_dimension=1, tiled=T...]
    cond x0 -> x1, blocking collectives: none -> 63.5 us
    pallas_call x0 -> x6, Pallas kernels: none -> 26.3 us  [the longest x1 11.9 us: branch(): pl.pallas_call(partial(fock_kernel, 1.0 / scale), grid_spec=pltpu.Prefetc...]
    another operation x9 -> x1, loops' own time: 21.6 us -> 0.95 us  [local(): lax.switch(which, [partial(branch, c) for c in counts], received, integrals)]
    squeeze x16 -> x0, local copies, waits for them, and re-layouts: 19.1 us -> none  [the longest x8 10.4 us: slot_fock(): factors = integrals[position]]
    all_gather x1, waiting for transfers between devices: 47.2 us -> 28.5 us  [branch(): gathered = lax.all_gather(packed, ('tile', 'ka'), axis=0, tiled=True)]
    dot_general x17 -> x0, matrix products: 13.1 us -> none  [the longest x8 7.8 us: block_fock(): jnp.einsum('qij,ij->q', factor_block, density_block, preferred_element_ty...]
    dynamic_slice x17 -> x2, local copies, waits for them, and re-layouts: 10.6 us -> 1.37 us  [the longest x1 1.3 us: local(): own_sizes = lax.dynamic_slice_in_dim(sizes, first, per_group)]
  transfers between devices with their start and end apart: 6 -> 5, of which waited for: 4 -> 2; matrix products, arithmetic and copies ran while one was open for 5% -> 7% of each run, Pallas kernels for 0% -> 12%
where the time goes in v1:
time: 184 us
  blocking collectives  63.5 us (35%)
  waiting for transfers between devices  45.3 us (25%)
  Pallas kernels  26.3 us (14%)
  starting transfers between devices  16 us (9%)
  other arithmetic  14.6 us (8%)
  between operations  14.1 us (8%)
  local copies, waits for them, and re-layouts  2.87 us (2%)
    cond x1, blocking collectives  63.5 us
    all_gather x1, waiting for transfers between devices, branch(): gathered = lax.all_gather(packed, ('tile', 'ka'), axis=0, tiled=True)  28.5 us
    all_to_all x1, waiting for transfers between devices, local(): lax.all_to_all(outgoing.reshape(groups, capacity, slab, basis), 'frag', s...  16.8 us
    pallas_call x1, Pallas kernels, branch(): pl.pallas_call(partial(fock_kernel, 1.0 / scale), grid_spec=pltpu.Prefetc...  11.9 us
    pallas_call x1, Pallas kernels, local(): pl.pallas_call(base_kernel, grid_spec=pltpu.PrefetchScalarGridSpec(num_sc...  7.14 us
    ppermute x1, starting transfers between devices, local(): low = lax.ppermute(masked, 'frag', forward)  5.72 us
    all_to_all x1, starting transfers between devices, local(): lax.all_to_all(outgoing.reshape(groups, capacity, slab, basis), 'frag', s...  4.82 us
    all_to_all x1, starting transfers between devices, local(): lax.all_to_all(back.reshape(groups, capacity, slab, basis).astype(WIRE),...  4.15 us
  transfers between devices with their start and end apart: 5, of which 2 were waited for; matrix products, arithmetic and copies ran while one was open for 7% of the time, Pallas kernels for 12%

profile of v1, /device:TPU:0, one launch (start us, length us, event | category | flops | bytes accessed | tf_op | source)
XLA Modules:
  0.0 183.5 jit_solution(4122792300131084357)
XLA Ops:
  6.5 0.8 select_reduce_fusion.5
  7.4 0.2 convert_reduce_fusion.1
  7.6 0.7 select_reduce_fusion.4.pick_ref
  8.3 1.3 dynamic_slice.9.size_ref
  9.6 2.2 %prep.1 = (bf16[8,64,512]{2,1,0:T(8,128)(2,1)}, bf16[8,64,512]{2,1,0:T(8,128)(2,1)}) custom-call(s32[8]{0:T(128)} %dynamic_slice.9.size_ref, s32[8]{0:T(128)} %select_reduce_fusion.4.pick_ref, s32[1]{0:T(128)} %bitcast.15.row_ref, bf16[8,64,512]{2,1,0:T(8,128)(2,1)} %d_ref.1), custom_call_target="tpu_custom_call" | custom-call | tf_op jit(solution)/shard_map/prep/pallas_call | solution.py:159
  11.7 5.7 %collective-permute-start = (bf16[8,64,512]{2,1,0:T(8,128)(2,1)}, bf16[8,64,512]{2,1,0:T(8,128)(2,1)}, u32[]{:S(2)}, u32[]{:S(2)}) collective-permute-start(bf16[8,64,512]{2,1,0:T(8,128)(2,1)} %get-tuple-element.133.mid_ref), channel_id=1, source_target_pairs={{0,8},{8,16},{16,24},{1,9},{9,17},{17,25},{2,10},{10,18},{18,26},{... | collective-permute-start | bytes 1572872 | tf_op jit(solution)/shard_map/ppermute | solution.py:173
  17.4 1.3 collective-permute-start.1
  18.7 4.8 %all-to-all-start = ((bf16[4,2,64,512]{3,2,1,0:T(8,128)(2,1)}), bf16[4,2,64,512]{3,2,1,0:T(8,128)(2,1)S(1)}, u32[]{:S(2)}, u32[]{:S(2)}) async-start(bf16[4,2,64,512]{3,2,1,0:T(8,128)(2,1)} %bitcast.62), calls=%async_computation | async-start | bytes 1048576 | tf_op jit(solution)/shard_map/all_to_all | solution.py:167
  23.5 0.7 and_select_fusion
  24.3 0.7 and_select_fusion.1
  24.9 0.8 select_reduce_fusion
  25.9 0.2 convert_reduce_fusion
  26.1 0.1 select_reduce_fusion.3
  26.3 0.1 reduce_sum.94
  26.4 0.7 reduce_max.9
  27.2 2.0 %fusion.2 = s32[]{:T(128)} fusion(s32[4]{0:T(128)} %constant.67.clone, s32[]{:T(128)} %reduce_max.9), kind=kLoop, calls=%fused_computation.37 | loop fusion | flops 11 | bytes 24 | tf_op jit(solution)/shard_map/reduce_sum | solution.py:239
  30.0 16.8 %all-to-all-done = bf16[4,2,64,512]{3,2,1,0:T(8,128)(2,1)S(1)} async-done(((bf16[4,2,64,512]{3,2,1,0:T(8,128)(2,1)}), bf16[4,2,64,512]{3,2,1,0:T(8,128)(2,1)S(1)}, u32[]{:S(2)}, u32[]{:S(2)}) %all-to-all-start) | async-done | bytes 524320 | tf_op jit(solution)/shard_map/all_to_all | solution.py:167
  46.8 113.1 %conditional.1 = (f32[8,64,512]{2,1,0:T(8,128)S(1)}) conditional(s32[]{:T(128)} %clamp.3, (s32[32]{0:T(128)S(1)}, s32[32]{0:T(128)S(1)}, bf16[8,64,512]{2,1,0:T(8,128)(2,1)S(1)}, s32[8]{0:T(128)S(1)}, s32[8]{0:T(128)S(1)}, /*index=5*/bf16[8,2,512,512]{3,2,1,0:T(8,128)(2,1)}, s32[8]{0:T(128)S(1)}, ...), branch_computations={%region_11.13_spmd, %region_13.15_spmd, %region_15.17_spmd, %regio... | conditional | flops 3407875 | bytes 36700260 | solution.py:240
  46.8 1.3 pack.6
  48.2 1.3 dynamic-slice.2
  50.2 28.5 %all-gather.8.cloned.1.call-done = bf16[128,64,128]{2,1,0:T(8,128)(2,1)} async-done(((bf16[16,64,128]{2,1,0:T(8,128)(2,1)}), bf16[128,64,128]{2,1,0:T(8,128)(2,1)}) %all-gather.8.cloned.1.call-update) | async-done | bytes 2097168 | tf_op jit(solution)/shard_map/cond/branch_1_fun/all_gather | solution.py:204
  78.6 11.9 %fock.6 = f32[8,16,64,128]{3,2,1,0:T(8,128)} custom-call(s32[8]{0:T(128)S(1)} %get-tuple-element.101.cls_ref, s32[8]{0:T(128)S(1)} %get-tuple-element.102.off_ref, bf16[8,16,64,128]{3,2,1,0:T(8,128)(2,1)} %bitcast.59, bf16[8,2,512,512]{3,2,1,0:T(8,128)(2,1)} %get-tuple-element.106.l_ref), custom_call_target="tpu_custom_call" | custom-call | tf_op jit(solution)/shard_map/cond/branch_1_fun/fock/pallas_call | solution.py:206
  90.5 2.7 %convert_element_type.46 = f16[8,16,64,128]{3,2,1,0:T(8,128)(2,1)S(1)} convert(f32[8,16,64,128]{3,2,1,0:T(8,128)} %fock.6) | non-fusion elementwise | flops 1048576 | bytes 6291456 | tf_op jit(solution)/shard_map/cond/branch_1_fun/convert_element_type | solution.py:226
  93.2 63.5 %all-reduce.16 = u32[128,4,1024]{2,1,0:T(4,128)} all-reduce(u32[128,4,1024]{2,1,0:T(4,128)S(1)} %bitcast.50), channel_id=3, replica_groups=mesh['frag'=4,'tile'=4,'ka'=2] {'tile','ka'}, use_global_device_ids=true, to_apply=%region_14.14.clone.clone | all-reduce | flops 524288 | bytes 4194304 | tf_op jit(solution)/shard_map/cond
  156.7 1.8 dynamic-slice_convert_fusion.1.p_ref
  158.5 1.2 unpack.6
  159.9 0.9 convert_element_type.68
  160.8 4.2 %all-to-all-start.1 = ((f16[4,2,64,512]{3,2,1,0:T(8,128)(2,1)}), f16[4,2,64,512]{3,2,1,0:T(8,128)(2,1)S(1)}, u32[]{:S(2)}, u32[]{:S(2)}) async-start(f16[4,2,64,512]{3,2,1,0:T(8,128)(2,1)} %bitcast.18), calls=%async_computation.1 | async-start | bytes 1048576 | tf_op jit(solution)/shard_map/all_to_all | solution.py:241
  165.1 0.6 broadcast_subtract_fusion.near_ref
  165.7 7.1 %base.1.b_ref = f32[8,64,512]{2,1,0:T(8,128)} custom-call(s32[8,4]{1,0:T(8,128)} %broadcast_subtract_fusion.near_ref, bf16[8,64,512]{2,1,0:T(8,128)(2,1)} %collective-permute-done.low_ref, bf16[8,64,512]{2,1,0:T(8,128)(2,1)} %get-tuple-element.133.mid_ref, bf16[8,64,512]{2,1,0:T(8,128)(2,1)} %collective-permute-done.1.high_ref, bf16[8,64,512]{2,1,0:T(8,128)(2,1)} %h_ref.1, ...), custom_call_target="tpu_custom_call" | custom-call | tf_op jit(solution)/shard_map/base/pallas_call | solution.py:179
  172.8 1.2 bitcast_convert_fusion.r_ref
  174.0 2.7 %final.1 = f32[8,64,512]{2,1,0:T(8,128)} custom-call(s32[8]{0:T(128)} %dynamic_slice.9.size_ref, s32[8]{0:T(128)} %copy-done.1, s32[1]{0:T(128)} %bitcast.15.row_ref, f32[8,64,512]{2,1,0:T(8,128)} %base.1.b_ref, f32[8,64,512]{2,1,0:T(8,128)} %bitcast_convert_fusion.r_ref), custom_call_target="tpu_custom_call" | custom-call | tf_op jit(solution)/shard_map/final/pallas_call | solution.py:244
  (19 shorter events, 0.5 us)
Async XLA Ops:
  7.6 39.2 %copy-start.1 = (s32[8]{0:T(128)}, s32[8]{0:T(128)S(1)}, u32[]{:S(2)}) copy-start(s32[8]{0:T(128)S(1)} %multiply_add_fusion.1.slot_ref) | copy-start | bytes 100
  11.7 154.0 %collective-permute-start = (bf16[8,64,512]{2,1,0:T(8,128)(2,1)}, bf16[8,64,512]{2,1,0:T(8,128)(2,1)}, u32[]{:S(2)}, u32[]{:S(2)}) collective-permute-start(bf16[8,64,512]{2,1,0:T(8,128)(2,1)} %get-tuple-element.133.mid_ref), channel_id=1, source_target_pairs={{0,8},{8,16},{16,24},{1,9},{9,17},{17,25},{2,10},{10,18},{18,26},{... | collective-permute-start | bytes 1572872 | tf_op jit(solution)/shard_map/ppermute | solution.py:173
  17.4 148.2 %collective-permute-start.1 = (bf16[8,64,512]{2,1,0:T(8,128)(2,1)}, bf16[8,64,512]{2,1,0:T(8,128)(2,1)}, u32[]{:S(2)}, u32[]{:S(2)}) collective-permute-start(bf16[8,64,512]{2,1,0:T(8,128)(2,1)} %get-tuple-element.133.mid_ref), channel_id=1, source_target_pairs={{8,0},{16,8},{24,16},{9,1},{17,9},{25,17},{10,2},{18,10},{26,18},{... | collective-permute-start | bytes 1572872 | tf_op jit(solution)/shard_map/ppermute | solution.py:174
  18.7 28.1 %all-to-all-start = ((bf16[4,2,64,512]{3,2,1,0:T(8,128)(2,1)}), bf16[4,2,64,512]{3,2,1,0:T(8,128)(2,1)S(1)}, u32[]{:S(2)}, u32[]{:S(2)}) async-start(bf16[4,2,64,512]{3,2,1,0:T(8,128)(2,1)} %bitcast.62), calls=%async_computation | async-start | bytes 1048576 | tf_op jit(solution)/shard_map/all_to_all | solution.py:167
  46.8 118.2 %copy-start = (s32[8,4]{0,1:T(4,128)S(1)}, s32[8,4]{0,1:T(4,128)}, u32[]{:S(2)}) copy-start(s32[8,4]{0,1:T(4,128)} %param.14) | copy-start | bytes 388
  46.8 31.8 %all-gather.8.cloned.1.call-start = ((), (), s32[]{:S(2)}) async-start(), calls=%async_computation.3 | async-start | bytes 2359296 | tf_op jit(solution)/shard_map/cond/branch_1_fun/all_gather | solution.py:204
  160.8 12.0 %all-to-all-start.1 = ((f16[4,2,64,512]{3,2,1,0:T(8,128)(2,1)}), f16[4,2,64,512]{3,2,1,0:T(8,128)(2,1)S(1)}, u32[]{:S(2)}, u32[]{:S(2)}) async-start(f16[4,2,64,512]{3,2,1,0:T(8,128)(2,1)} %bitcast.18), calls=%async_computation.1 | async-start | bytes 1048576 | tf_op jit(solution)/shard_map/all_to_all | solution.py:241
Sparse Core Ops, SparseCore 0:
  49.2 29.3 all-gather.7
